TPU v7x, 512 devices: a whole 4x4x16 slice. The times are simulated.
512 devices in a mesh: blk: 32 (over y, x, core), mpo: 16 (over z).
Axes of the slice: x: 4, y: 4, z: 16, core: 2. Of those that a mesh axis runs over, the one named last changes fastest.
Arguments:
- theta: float32 [64, 128, 16, 128], P('blk'), may hold values from -6 to 6
- block_dims: int32 [64, 2], P('blk'), may hold values from 32 to 128, as said below
- pair_mask: int32 [96, 64], P(None, 'blk'), may hold values 0 or 1
- term_charge: int32 [96], replicated, may hold values from -1 to 1
- left_env: float32 [96, 64, 128, 128], P('mpo', 'blk'), may hold values from -0.5 to 0.5
- right_env: float32 [96, 64, 128, 128], P('mpo', 'blk'), may hold values from -0.5 to 0.5
- site_one: float32 [96, 4, 4], replicated, may hold values from -0.3125 to 0.3125
- site_two: float32 [96, 4, 4], replicated, may hold values from -3 to 3
Outputs:
- hpsi: float32 [64, 128, 16, 128], P('blk', 'mpo')
Inputs may be any that keep to these rules, and one draw needn't show every extreme that they name: `block_dims`: kept dimensions of each sector; rows and columns of a block beyond them are empty. The first sector keeps 128 on both sides.
All inputs are finite; a program needn't handle non-finite values. No bound on the sum of `pair_mask` on one device may be relied on, other than what follows from the above.
Results may differ from a plain program's by a relative error of at most 0.0003.
Values sent between devices are 32-bit elements; how exact they have to be, the bound alone decides.
A program may use at most 64 MiB of HBM per device.

v0:
```python
import jax
import jax.numpy as jnp
from jax import lax
from jax.sharding import PartitionSpec as P


def extended(cells, sides, width):
    for axis, dim in sides:
        count = lax.axis_size(axis)
        ends = count - 1
        head = lax.slice_in_dim(cells, 0, width, axis=dim)
        tail = lax.slice_in_dim(cells, cells.shape[dim] - width, cells.shape[dim], axis=dim)
        cells = jnp.concatenate(
            [
                lax.ppermute(tail, axis, [(i, (i + 1) % count) for i in range(ends)]),
                cells,
                lax.ppermute(head, axis, [((i + 1) % count, i) for i in range(ends)]),
            ],
            axis=dim,
        )
    return cells


def sector_mask(block_dims, bond_cap):
    positions = jnp.arange(bond_cap, dtype=jnp.int32)
    left_ok = positions[None, :] < block_dims[:, 0:1]
    right_ok = positions[None, :] < block_dims[:, 1:2]
    return (left_ok[:, :, None] & right_ok[:, None, :]).astype(jnp.float32)


def make_pair(first_op, second_op):
    states = first_op.shape[0]
    return (first_op[:, None, :, None] * second_op[None, :, None, :]).reshape(
        states * states, states * states
    )


def apply_term(left_rows, source, site_pair, right_block):
    highest = lax.Precision.HIGHEST
    row_count = left_rows.shape[0]
    moved = jnp.dot(
        left_rows,
        source.reshape(source.shape[0], -1),
        precision=highest,
        preferred_element_type=jnp.float32,
    )
    moved = moved.reshape(row_count, source.shape[1], source.shape[2])
    mixed = jnp.einsum("pq,aqd->apd", site_pair, moved, precision=highest)
    return jnp.einsum("apd,bd->apb", mixed, right_block, precision=highest)


def all_sectors(running, padded, left_all, right_all, charge, site_pair, allowed):
    sectors = left_all.shape[0]
    source_index = jnp.arange(sectors, dtype=jnp.int32) + 1 - charge

    def per_sector(left_rows, index, right_block):
        source = lax.dynamic_index_in_dim(padded, index, 0, keepdims=False)
        return apply_term(left_rows, source, site_pair, right_block)

    terms = jax.vmap(per_sector)(left_all, source_index, right_all)
    return running + allowed.astype(jnp.float32)[:, None, None, None] * terms


def body(theta, block_dims, pair_mask, term_charge, left_env, right_env, site_one, site_two):
    bond_cap = theta.shape[1]
    group_index = lax.axis_index("mpo")
    group_count = lax.axis_size("mpo")
    row_count = bond_cap // group_count
    first_row = group_index * row_count
    block_mask = sector_mask(block_dims, bond_cap)
    masked = theta * block_mask[:, :, None, :]
    padded = extended(masked, (("blk", 0),), 1)
    row_mask = lax.dynamic_slice_in_dim(block_mask, first_row, row_count, 1)
    term_count = left_env.shape[0]
    first_term = group_index * term_count

    def local_term(w, running):
        term_index = first_term + w
        charge = lax.dynamic_index_in_dim(term_charge, term_index, 0, keepdims=False)
        allowed = lax.dynamic_index_in_dim(pair_mask, term_index, 0, keepdims=False)
        first_op = lax.dynamic_index_in_dim(site_one, term_index, 0, keepdims=False)
        second_op = lax.dynamic_index_in_dim(site_two, term_index, 0, keepdims=False)
        left_all = lax.dynamic_index_in_dim(left_env, w, 0, keepdims=False)
        right_all = lax.dynamic_index_in_dim(right_env, w, 0, keepdims=False)
        return all_sectors(
            running, padded, left_all, right_all, charge, make_pair(first_op, second_op), allowed
        )

    partial_value = lax.fori_loop(0, term_count, local_term, jnp.zeros(theta.shape, jnp.float32))
    whole_sum = lax.psum(partial_value, "mpo")
    mine = lax.dynamic_slice_in_dim(whole_sum, first_row, row_count, 1)
    return mine * row_mask[:, :, None, :]


def solution(mesh):
    placed = (
        P("blk", None, None, None),
        P("blk", None),
        P(None, "blk"),
        P(),
        P("mpo", "blk", None, None),
        P("mpo", "blk", None, None),
        P(),
        P(),
    )
    return jax.shard_map(
        body, mesh=mesh, in_specs=placed, out_specs=P("blk", "mpo", None, None), check_vma=False
    )
```

profile of v0, /device:TPU:2, one launch (start us, length us, event | category | flops | bytes accessed | tf_op | source)
XLA Modules:
  0.0 307.2 jit_solution(4016067030616916532)
XLA Ops:
  6.5 1.0 slice_reduce_fusion.1
  7.7 2.2 copy_multiply_fusion
  10.0 1.2 fusion.20
  11.1 1.9 collective-permute-start
  13.1 3.6 %collective-permute-start.1 = (f32[1,128,16,128]{3,1,2,0:T(8,128)S(1)}, f32[1,128,16,128]{3,1,2,0:T(8,128)}, u32[]{:S(2)}, u32[]{:S(2)}) collective-permute-start(f32[1,128,16,128]{3,1,2,0:T(8,128)S(1)} %get-tuple-element.253), channel_id=1, source_target_pairs={{16,0},{32,16},{48,32},{64,48},{80,64},{96,80},{112,96},{128,112},... | collective-permute-start | bytes 3145736 | tf_op jit(solution)/shard_map/ppermute | solution.py:17
  17.8 9.7 %collective-permute-done = f32[1,128,16,128]{3,1,2,0:T(8,128)} collective-permute-done((f32[1,128,16,128]{3,1,2,0:T(8,128)}, f32[1,128,16,128]{3,1,2,0:T(8,128)}, u32[]{:S(2)}, u32[]{:S(2)}) %collective-permute-start) | collective-permute-done | bytes 1048608 | tf_op jit(solution)/shard_map/ppermute | solution.py:15
  27.6 1.4 collective-permute-done.1
  29.0 4.0 %pad_maximum_fusion = f32[4,128,16,128]{3,1,2,0:T(8,128)} fusion(f32[1,128,16,128]{3,1,2,0:T(8,128)} %collective-permute-done.1, f32[2,128,16,128]{3,1,2,0:T(8,128)S(1)} %copy_multiply_fusion, f32[1,128,16,128]{3,1,2,0:T(8,128)} %collective-permute-done), kind=kLoop, calls=%fused_computation.25 | loop fusion | flops 2097152 | bytes 8388608 | tf_op jit(solution)/shard_map/concatenate | solution.py:13
  33.0 109.8 %while.14 = (s32[]{:T(128)}, f32[2,128,16,128]{3,1,2,0:T(8,128)}, s32[]{:T(128)}, s32[96,2]{1,0:T(8,128)S(1)}, f32[6,2,128,128]{3,2,1,0:T(8,128)}, /*index=5*/s3...) while((s32[]{:T(128)}, f32[2,128,16,128]{3,1,2,0:T(8,128)}, ...), condition=%wide.region_1.2_spmd.clone, body=%wide.region_0.1_spmd.clone.sunk | while | flops 1712849152 | bytes 44307156 | solution.py:89
  35.0 2.9 gather_fusion
  37.8 1.9 copy.37
  39.7 3.6 %fusion.37 = f32[2,128,2048]{2,1,0:T(8,128)S(1)} fusion(f32[2,128,2048]{1,2,0:T(8,128)} %bitcast.61, f32[6,2,128,128]{3,2,1,0:T(8,128)} %get-tuple-element.351, s32[]{:T(128)S(6)} %copy.41), kind=kOutput, calls=%fused_computation.8.clone.1 | convolution fusion | flops 805306368 | bytes 4325380 | tf_op jit(solution)/shard_map/while/body/eval_jaxpr/vmap()/dot_general | solution.py:41
  43.7 1.9 fusion.38
  45.6 4.4 %select_add_fusion.2 = f32[2,128,16,128]{3,1,2,0:T(8,128)S(1)} fusion(f32[2,128,16,128]{3,1,2,0:T(8,128)S(1)} %copy-done, f32[2,128,128,16]{2,3,1,0:T(8,128)S(1)} %fusion.38, f32[2]{0:T(128)S(1)} %fusion.39, pred[]{:T(512)S(6)} %compare.3, f32[6,2,128,128]{3,2,1,0:T(8,128)} %get-tuple-element.356, s32[]{:T(128)S(6)} %copy.41), kind=kOutput, calls=%fused_computation.6.clone.1 | convolution fusion | flops 806879232 | bytes 6422541 | tf_op jit(solution)/shard_map/while/body/eval_jaxpr/vmap(apd,bd->apb)/dot_general | solution.py:49
  50.0 1.3 copy-done.1
  53.3 2.9 gather_fusion
  56.1 1.9 copy.37
  58.0 3.6 %fusion.37 = f32[2,128,2048]{2,1,0:T(8,128)S(1)} fusion(f32[2,128,2048]{1,2,0:T(8,128)} %bitcast.61, f32[6,2,128,128]{3,2,1,0:T(8,128)} %get-tuple-element.351, s32[]{:T(128)S(6)} %copy.41), kind=kOutput, calls=%fused_computation.8.clone.1 | convolution fusion | flops 805306368 | bytes 4325380 | tf_op jit(solution)/shard_map/while/body/eval_jaxpr/vmap()/dot_general | solution.py:41
  62.0 1.9 fusion.38
  63.9 4.4 %select_add_fusion.2 = f32[2,128,16,128]{3,1,2,0:T(8,128)S(1)} fusion(f32[2,128,16,128]{3,1,2,0:T(8,128)S(1)} %copy-done, f32[2,128,128,16]{2,3,1,0:T(8,128)S(1)} %fusion.38, f32[2]{0:T(128)S(1)} %fusion.39, pred[]{:T(512)S(6)} %compare.3, f32[6,2,128,128]{3,2,1,0:T(8,128)} %get-tuple-element.356, s32[]{:T(128)S(6)} %copy.41), kind=kOutput, calls=%fused_computation.6.clone.1 | convolution fusion | flops 806879232 | bytes 6422541 | tf_op jit(solution)/shard_map/while/body/eval_jaxpr/vmap(apd,bd->apb)/dot_general | solution.py:49
  68.3 1.3 copy-done.1
  71.6 2.9 gather_fusion
  74.4 1.9 copy.37
  76.3 3.6 %fusion.37 = f32[2,128,2048]{2,1,0:T(8,128)S(1)} fusion(f32[2,128,2048]{1,2,0:T(8,128)} %bitcast.61, f32[6,2,128,128]{3,2,1,0:T(8,128)} %get-tuple-element.351, s32[]{:T(128)S(6)} %copy.41), kind=kOutput, calls=%fused_computation.8.clone.1 | convolution fusion | flops 805306368 | bytes 4325380 | tf_op jit(solution)/shard_map/while/body/eval_jaxpr/vmap()/dot_general | solution.py:41
  80.3 1.9 fusion.38
  82.2 4.4 %select_add_fusion.2 = f32[2,128,16,128]{3,1,2,0:T(8,128)S(1)} fusion(f32[2,128,16,128]{3,1,2,0:T(8,128)S(1)} %copy-done, f32[2,128,128,16]{2,3,1,0:T(8,128)S(1)} %fusion.38, f32[2]{0:T(128)S(1)} %fusion.39, pred[]{:T(512)S(6)} %compare.3, f32[6,2,128,128]{3,2,1,0:T(8,128)} %get-tuple-element.356, s32[]{:T(128)S(6)} %copy.41), kind=kOutput, calls=%fused_computation.6.clone.1 | convolution fusion | flops 806879232 | bytes 6422541 | tf_op jit(solution)/shard_map/while/body/eval_jaxpr/vmap(apd,bd->apb)/dot_general | solution.py:49
  86.6 1.3 copy-done.1
  89.9 2.9 gather_fusion
  92.8 1.9 copy.37
  94.6 3.6 %fusion.37 = f32[2,128,2048]{2,1,0:T(8,128)S(1)} fusion(f32[2,128,2048]{1,2,0:T(8,128)} %bitcast.61, f32[6,2,128,128]{3,2,1,0:T(8,128)} %get-tuple-element.351, s32[]{:T(128)S(6)} %copy.41), kind=kOutput, calls=%fused_computation.8.clone.1 | convolution fusion | flops 805306368 | bytes 4325380 | tf_op jit(solution)/shard_map/while/body/eval_jaxpr/vmap()/dot_general | solution.py:41
  98.6 1.9 fusion.38
  100.5 4.4 %select_add_fusion.2 = f32[2,128,16,128]{3,1,2,0:T(8,128)S(1)} fusion(f32[2,128,16,128]{3,1,2,0:T(8,128)S(1)} %copy-done, f32[2,128,128,16]{2,3,1,0:T(8,128)S(1)} %fusion.38, f32[2]{0:T(128)S(1)} %fusion.39, pred[]{:T(512)S(6)} %compare.3, f32[6,2,128,128]{3,2,1,0:T(8,128)} %get-tuple-element.356, s32[]{:T(128)S(6)} %copy.41), kind=kOutput, calls=%fused_computation.6.clone.1 | convolution fusion | flops 806879232 | bytes 6422541 | tf_op jit(solution)/shard_map/while/body/eval_jaxpr/vmap(apd,bd->apb)/dot_general | solution.py:49
  104.9 1.3 copy-done.1
  108.2 2.9 gather_fusion
  111.1 1.9 copy.37
  112.9 3.6 %fusion.37 = f32[2,128,2048]{2,1,0:T(8,128)S(1)} fusion(f32[2,128,2048]{1,2,0:T(8,128)} %bitcast.61, f32[6,2,128,128]{3,2,1,0:T(8,128)} %get-tuple-element.351, s32[]{:T(128)S(6)} %copy.41), kind=kOutput, calls=%fused_computation.8.clone.1 | convolution fusion | flops 805306368 | bytes 4325380 | tf_op jit(solution)/shard_map/while/body/eval_jaxpr/vmap()/dot_general | solution.py:41
  116.9 1.9 fusion.38
  118.8 4.4 %select_add_fusion.2 = f32[2,128,16,128]{3,1,2,0:T(8,128)S(1)} fusion(f32[2,128,16,128]{3,1,2,0:T(8,128)S(1)} %copy-done, f32[2,128,128,16]{2,3,1,0:T(8,128)S(1)} %fusion.38, f32[2]{0:T(128)S(1)} %fusion.39, pred[]{:T(512)S(6)} %compare.3, f32[6,2,128,128]{3,2,1,0:T(8,128)} %get-tuple-element.356, s32[]{:T(128)S(6)} %copy.41), kind=kOutput, calls=%fused_computation.6.clone.1 | convolution fusion | flops 806879232 | bytes 6422541 | tf_op jit(solution)/shard_map/while/body/eval_jaxpr/vmap(apd,bd->apb)/dot_general | solution.py:49
  123.2 1.3 copy-done.1
  126.5 2.9 gather_fusion
  129.4 1.9 copy.37
  131.2 3.6 %fusion.37 = f32[2,128,2048]{2,1,0:T(8,128)S(1)} fusion(f32[2,128,2048]{1,2,0:T(8,128)} %bitcast.61, f32[6,2,128,128]{3,2,1,0:T(8,128)} %get-tuple-element.351, s32[]{:T(128)S(6)} %copy.41), kind=kOutput, calls=%fused_computation.8.clone.1 | convolution fusion | flops 805306368 | bytes 4325380 | tf_op jit(solution)/shard_map/while/body/eval_jaxpr/vmap()/dot_general | solution.py:41
  135.2 1.9 fusion.38
  137.1 4.4 %select_add_fusion.2 = f32[2,128,16,128]{3,1,2,0:T(8,128)S(1)} fusion(f32[2,128,16,128]{3,1,2,0:T(8,128)S(1)} %copy-done, f32[2,128,128,16]{2,3,1,0:T(8,128)S(1)} %fusion.38, f32[2]{0:T(128)S(1)} %fusion.39, pred[]{:T(512)S(6)} %compare.3, f32[6,2,128,128]{3,2,1,0:T(8,128)} %get-tuple-element.356, s32[]{:T(128)S(6)} %copy.41), kind=kOutput, calls=%fused_computation.6.clone.1 | convolution fusion | flops 806879232 | bytes 6422541 | tf_op jit(solution)/shard_map/while/body/eval_jaxpr/vmap(apd,bd->apb)/dot_general | solution.py:49
  141.5 1.3 copy-done.1
  142.8 4.2 %copy.20 = f32[2,128,16,128]{3,2,1,0:T(8,128)} copy(f32[2,128,16,128]{3,1,2,0:T(8,128)} %get-tuple-element.174) | data formatting | bytes 4194304 | tf_op jit(solution)/shard_map/while | solution.py:89
  147.0 151.8 %all-reduce.2.cloned.1.call-done = f32[2,128,16,128]{3,2,1,0:T(8,128)} async-done(((f32[2,128,16,128]{3,2,1,0:T(8,128)}), f32[2,128,16,128]{3,2,1,0:T(8,128)}) %all-reduce.2.cloned.1.call-update) | async-done | bytes 2097168 | tf_op jit(solution)/shard_map/psum | solution.py:90
  298.8 1.6 dynamic-slice_multiply_fusion
  (77 shorter events, 15.4 us)
Async XLA Ops:
  6.5 292.3 %all-reduce.2.cloned.1.call-start = ((), (), s32[]{:S(2)}) async-start(), calls=%async_computation | async-start | bytes 4194304 | tf_op jit(solution)/shard_map/psum | solution.py:90
  9.9 6.8 %copy-start.4 = (s32[96,2]{0,1:T(2,128)S(1)}, s32[96,2]{0,1:T(2,128)}, u32[]{:S(2)}) copy-start(s32[96,2]{0,1:T(2,128)} %param.12) | copy-start | bytes 2308
  10.0 6.9 %copy-start.2 = (f32[96,4,4]{0,2,1:T(4,128)S(1)}, f32[96,4,4]{0,2,1:T(4,128)}, u32[]{:S(2)}) copy-start(f32[96,4,4]{0,2,1:T(4,128)} %param.16) | copy-start | bytes 18436
  10.0 7.0 %copy-start.3 = (f32[96,4,4]{0,2,1:T(4,128)S(1)}, f32[96,4,4]{0,2,1:T(4,128)}, u32[]{:S(2)}) copy-start(f32[96,4,4]{0,2,1:T(4,128)} %param.17) | copy-start | bytes 18436
  11.1 16.4 %collective-permute-start = (f32[1,128,16,128]{3,1,2,0:T(8,128)}, f32[1,128,16,128]{3,1,2,0:T(8,128)}, u32[]{:S(2)}, u32[]{:S(2)}) collective-permute-start(f32[1,128,16,128]{3,1,2,0:T(8,128)} %get-tuple-element.252), channel_id=1, source_target_pairs={{0,16},{16,32},{32,48},{48,64},{64,80},{80,96},{96,112},{112,128},... | collective-permute-start | bytes 3145736 | tf_op jit(solution)/shard_map/ppermute | solution.py:15
  13.1 15.9 %collective-permute-start.1 = (f32[1,128,16,128]{3,1,2,0:T(8,128)S(1)}, f32[1,128,16,128]{3,1,2,0:T(8,128)}, u32[]{:S(2)}, u32[]{:S(2)}) collective-permute-start(f32[1,128,16,128]{3,1,2,0:T(8,128)S(1)} %get-tuple-element.253), channel_id=1, source_target_pairs={{16,0},{32,16},{48,32},{64,48},{80,64},{96,80},{112,96},{128,112},... | collective-permute-start | bytes 3145736 | tf_op jit(solution)/shard_map/ppermute | solution.py:17
  17.8 15.1 %copy-start.5 = (s32[96]{0:T(128)S(1)}, s32[96]{0:T(128)}, u32[]{:S(2)}) copy-start(s32[96]{0:T(128)} %param.13) | copy-start | bytes 1156
  43.7 1.9 copy-start
  49.9 1.3 copy-start.1
  62.0 1.9 copy-start
  68.3 1.3 copy-start.1
  80.3 1.9 copy-start
  86.6 1.3 copy-start.1
  98.6 1.9 copy-start
  104.9 1.3 copy-start.1
  116.9 1.9 copy-start
  123.2 1.3 copy-start.1
  135.2 1.9 copy-start
  141.5 1.3 copy-start.1
Sparse Core Ops, SparseCore 0:
  147.1 151.6 all-reduce.1
where the time goes:
time: 308 us; the launch traced here: 307 us
  waiting for transfers between devices  163 us (53%)
  matrix products  58.9 us (19%)
  local copies, waits for them, and re-layouts  53.9 us (18%)
  between operations  13.5 us (4%)
  other arithmetic  11.8 us (4%)
  starting transfers between devices  5.55 us (2%)
    psum x1, waiting for transfers between devices, body(): whole_sum = lax.psum(partial_value, 'mpo')  152 us
    gather x12, local copies, waits for them, and re-layouts, per_sector(): source = lax.dynamic_index_in_dim(padded, index, 0, keepdims=False)  28.4 us
    dot_general x6, matrix products, apply_term(): return jnp.einsum('apd,bd->apb', mixed, right_block, precision=highest)  26.2 us
    dot_general x6, matrix products, apply_term(): jnp.dot(left_rows, source.reshape(source.shape[0], -1), precision=highest...  21.4 us
    dot_general x6, matrix products, apply_term(): mixed = jnp.einsum('pq,aqd->apd', site_pair, moved, precision=highest)  11.3 us
    while x30, local copies, waits for them, and re-layouts  10.3 us
    ppermute x1, waiting for transfers between devices, extended(): lax.ppermute(tail, axis, [(i, (i + 1) % count) for i in range(ends)])  9.72 us
  transfers between devices with their start and end apart: 3, of which 3 were waited for; matrix products, arithmetic and copies ran while one was open for 0% of the time, Pallas kernels for 0%

commit v1 on v0

--- a/solution.py
+++ b/solution.py
@@ -2,6 +2,14 @@
 import jax.numpy as jnp
 from jax import lax
 from jax.sharding import PartitionSpec as P
+
+
+def add_in_pairs(x, mesh_axis):
+    size, summed = (lax.axis_size(mesh_axis), x)
+    for far in [1 << k for k in range(size.bit_length() - 1)]:
+        route = [(i, i ^ far) for i in range(size)]
+        summed = summed + lax.ppermute(summed, mesh_axis, route)
+    return summed
 
 
 def extended(cells, sides, width):
@@ -87,7 +95,7 @@
         )
 
     partial_value = lax.fori_loop(0, term_count, local_term, jnp.zeros(theta.shape, jnp.float32))
-    whole_sum = lax.psum(partial_value, "mpo")
+    whole_sum = add_in_pairs(partial_value, "mpo")
     mine = lax.dynamic_slice_in_dim(whole_sum, first_row, row_count, 1)
     return mine * row_mask[:, :, None, :]
 

time: 308 us -> 719 us (2.33)
  the two profiles are of different devices: /device:TPU:2 before, /device:TPU:10 now
where the time goes in v1:
time: 719 us; the launch traced here: 718 us
  waiting for transfers between devices  464 us (65%)
  starting transfers between devices  127 us (18%)
  matrix products  59.1 us (8%)
  local copies, waits for them, and re-layouts  53.2 us (7%)
  other arithmetic  14 us (2%)
    ppermute x4, waiting for transfers between devices, add_in_pairs(): summed = summed + lax.ppermute(summed, mesh_axis, route)  453 us
    ppermute x4, starting transfers between devices, add_in_pairs(): summed = summed + lax.ppermute(summed, mesh_axis, route)  122 us
    gather x12, local copies, waits for them, and re-layouts, per_sector(): source = lax.dynamic_index_in_dim(padded, index, 0, keepdims=False)  28.4 us
    dot_general x6, matrix products, apply_term(): return jnp.einsum('apd,bd->apb', mixed, right_block, precision=highest)  26.2 us
    dot_general x6, matrix products, apply_term(): jnp.dot(left_rows, source.reshape(source.shape[0], -1), precision=highest...  21.4 us
  transfers between devices with their start and end apart: 6, of which 6 were waited for; matrix products, arithmetic and copies ran while one was open for 0% of the time, Pallas kernels for 0%

profile of v1, /device:TPU:10, one launch (start us, length us, event | category | flops | bytes accessed | tf_op | source)
XLA Modules:
  0.0 718.0 jit_solution(10887411765942785940)
XLA Ops:
  1.2 2.2 copy_multiply_fusion
  4.6 1.9 collective-permute-start
  6.5 3.6 collective-permute-start.1
  11.3 9.7 %collective-permute-done = f32[1,128,16,128]{3,1,2,0:T(8,128)} collective-permute-done((f32[1,128,16,128]{3,1,2,0:T(8,128)}, f32[1,128,16,128]{3,1,2,0:T(8,128)}, u32[]{:S(2)}, u32[]{:S(2)}) %collective-permute-start) | collective-permute-done | bytes 1048608 | tf_op jit(solution)/shard_map/ppermute | solution.py:23
  21.0 1.4 collective-permute-done.1
  22.5 3.9 pad_maximum_fusion
  26.3 111.0 %while.14 = (s32[]{:T(128)}, f32[2,128,16,128]{3,1,2,0:T(8,128)}, s32[]{:T(128)}, s32[96,2]{1,0:T(8,128)S(1)}, f32[6,2,128,128]{3,2,1,0:T(8,128)}, /*index=5*/s3...) while((s32[]{:T(128)}, f32[2,128,16,128]{3,1,2,0:T(8,128)}, ...), condition=%wide.region_1.2_spmd.clone, body=%wide.region_0.1_spmd.clone.sunk | while | flops 1712849152 | bytes 44307156 | solution.py:97
  28.5 2.9 gather_fusion
  31.4 1.9 copy.40
  33.2 3.6 fusion.38
  37.2 1.9 fusion.39
  39.1 4.4 select_add_fusion.2
  47.0 2.9 gather_fusion
  49.9 1.9 copy.40
  51.7 3.6 fusion.38
  55.7 1.9 fusion.39
  57.6 4.4 select_add_fusion.2
  62.0 1.3 copy-done.1
  65.5 2.9 gather_fusion
  68.4 1.9 copy.40
  70.2 3.6 fusion.38
  74.2 1.9 fusion.39
  76.2 4.4 select_add_fusion.2
  84.0 2.9 gather_fusion
  86.9 1.9 copy.40
  88.7 3.6 fusion.38
  92.7 1.9 fusion.39
  94.7 4.4 select_add_fusion.2
  102.5 2.9 gather_fusion
  105.3 1.9 copy.40
  107.2 3.6 fusion.38
  111.2 1.9 fusion.39
  113.1 4.4 select_add_fusion.2
  121.0 2.9 gather_fusion
  123.9 1.9 copy.40
  125.7 3.6 fusion.38
  129.7 1.9 fusion.39
  131.6 4.4 select_add_fusion.2
  137.3 3.0 copy.22
  140.3 4.0 collective-permute-start.2
  144.3 45.3 %collective-permute-done.2 = f32[2,128,16,128]{3,2,1,0:T(8,128)S(1)} collective-permute-done((f32[2,128,16,128]{3,2,1,0:T(8,128)S(1)}, f32[2,128,16,128]{3,2,1,0:T(8,128)S(1)}, u32[]{:S(2)}, u32[]{:S(2)}) %collective-permute-start.2) | collective-permute-done | bytes 2097184 | tf_op jit(solution)/shard_map/ppermute | solution.py:11
  190.8 5.2 collective-permute-start.3
  196.0 91.2 %collective-permute-done.3 = f32[2,128,16,128]{3,2,1,0:T(8,128)S(1)} collective-permute-done((f32[2,128,16,128]{3,2,1,0:T(8,128)S(1)}, f32[2,128,16,128]{3,2,1,0:T(8,128)S(1)}, u32[]{:S(2)}, u32[]{:S(2)}) %collective-permute-start.3) | collective-permute-done | bytes 2097184 | tf_op jit(solution)/shard_map/ppermute | solution.py:11
  287.5 9.2 %collective-permute-start.4 = (f32[2,128,16,128]{3,2,1,0:T(8,128)S(1)}, f32[2,128,16,128]{3,2,1,0:T(8,128)S(1)}, u32[]{:S(2)}, u32[]{:S(2)}) collective-permute-start(f32[2,128,16,128]{3,2,1,0:T(8,128)S(1)} %add.96), channel_id=1, source_target_pairs={{0,4},{1,5},{2,6},{3,7},{4,0},{5,1},{6,2},{7,3},{8,12},{9,13},{10,... | collective-permute-start | bytes 6291464 | tf_op jit(solution)/shard_map/ppermute | solution.py:11
  296.7 225.2 %collective-permute-done.4 = f32[2,128,16,128]{3,2,1,0:T(8,128)S(1)} collective-permute-done((f32[2,128,16,128]{3,2,1,0:T(8,128)S(1)}, f32[2,128,16,128]{3,2,1,0:T(8,128)S(1)}, u32[]{:S(2)}, u32[]{:S(2)}) %collective-permute-start.4) | collective-permute-done | bytes 2097184 | tf_op jit(solution)/shard_map/ppermute | solution.py:11
  522.2 103.1 %collective-permute-start.5 = (f32[2,128,16,128]{3,2,1,0:T(8,128)S(1)}, f32[2,128,16,128]{3,2,1,0:T(8,128)}, u32[]{:S(2)}, u32[]{:S(2)}) collective-permute-start(f32[2,128,16,128]{3,2,1,0:T(8,128)S(1)} %add.97), channel_id=1, source_target_pairs={{0,8},{1,9},{2,10},{3,11},{4,12},{5,13},{6,14},{7,15},{8,0},{9,1},... | collective-permute-start | bytes 6291464 | tf_op jit(solution)/shard_map/ppermute | solution.py:11
  625.3 91.1 %collective-permute-done.5 = f32[2,128,16,128]{3,2,1,0:T(8,128)} collective-permute-done((f32[2,128,16,128]{3,2,1,0:T(8,128)S(1)}, f32[2,128,16,128]{3,2,1,0:T(8,128)}, u32[]{:S(2)}, u32[]{:S(2)}) %collective-permute-start.5) | collective-permute-done | bytes 2097184 | tf_op jit(solution)/shard_map/ppermute | solution.py:11
  716.4 1.6 fusion.20
  (87 shorter events, 26.9 us)
Async XLA Ops:
  3.4 6.8 copy-start.5
  3.4 6.9 copy-start.3
  3.4 7.0 copy-start.4
  4.6 16.4 %collective-permute-start = (f32[1,128,16,128]{3,1,2,0:T(8,128)}, f32[1,128,16,128]{3,1,2,0:T(8,128)}, u32[]{:S(2)}, u32[]{:S(2)}) collective-permute-start(f32[1,128,16,128]{3,1,2,0:T(8,128)} %get-tuple-element.252), channel_id=1, source_target_pairs={{0,16},{16,32},{32,48},{48,64},{64,80},{80,96},{96,112},{112,128},... | collective-permute-start | bytes 3145736 | tf_op jit(solution)/shard_map/ppermute | solution.py:23
  6.5 15.9 %collective-permute-start.1 = (f32[1,128,16,128]{3,1,2,0:T(8,128)S(1)}, f32[1,128,16,128]{3,1,2,0:T(8,128)}, u32[]{:S(2)}, u32[]{:S(2)}) collective-permute-start(f32[1,128,16,128]{3,1,2,0:T(8,128)S(1)} %get-tuple-element.253), channel_id=1, source_target_pairs={{16,0},{32,16},{48,32},{64,48},{80,64},{96,80},{112,96},{128,112},... | collective-permute-start | bytes 3145736 | tf_op jit(solution)/shard_map/ppermute | solution.py:25
  11.3 15.0 %copy-start.6 = (s32[96]{0:T(128)S(1)}, s32[96]{0:T(128)}, u32[]{:S(2)}) copy-start(s32[96]{0:T(128)} %param.13) | copy-start | bytes 1156
  37.2 1.9 copy-start
  43.5 1.3 copy-start.1
  55.7 1.9 copy-start
  62.0 1.3 copy-start.1
  74.2 1.9 copy-start
  80.5 1.3 copy-start.1
  92.7 1.9 copy-start
  99.0 1.3 copy-start.1
  111.2 1.9 copy-start
  117.5 1.3 copy-start.1
  129.7 1.9 copy-start
  136.0 1.3 copy-start.1
  137.3 52.3 %copy-start.2 = (f32[2,128,16,128]{3,1,2,0:T(8,128)S(1)}, f32[2,128,16,128]{3,1,2,0:T(8,128)}, u32[]{:S(2)}) copy-start(f32[2,128,16,128]{3,1,2,0:T(8,128)} %get-tuple-element.174) | copy-start | bytes 6291460
  140.3 49.3 %collective-permute-start.2 = (f32[2,128,16,128]{3,2,1,0:T(8,128)S(1)}, f32[2,128,16,128]{3,2,1,0:T(8,128)S(1)}, u32[]{:S(2)}, u32[]{:S(2)}) collective-permute-start(f32[2,128,16,128]{3,2,1,0:T(8,128)S(1)} %copy.22), channel_id=1, source_target_pairs={{0,1},{1,0},{2,3},{3,2},{4,5},{5,4},{6,7},{7,6},{8,9},{9,8},{10,11... | collective-permute-start | bytes 6291464 | tf_op jit(solution)/shard_map/ppermute | solution.py:11
  190.8 96.4 %collective-permute-start.3 = (f32[2,128,16,128]{3,2,1,0:T(8,128)S(1)}, f32[2,128,16,128]{3,2,1,0:T(8,128)S(1)}, u32[]{:S(2)}, u32[]{:S(2)}) collective-permute-start(f32[2,128,16,128]{3,2,1,0:T(8,128)S(1)} %copy_add_fusion), channel_id=1, source_target_pairs={{0,2},{1,3},{2,0},{3,1},{4,6},{5,7},{6,4},{7,5},{8,10},{9,11},{10,... | collective-permute-start | bytes 6291464 | tf_op jit(solution)/shard_map/ppermute | solution.py:11
  287.5 234.4 %collective-permute-start.4 = (f32[2,128,16,128]{3,2,1,0:T(8,128)S(1)}, f32[2,128,16,128]{3,2,1,0:T(8,128)S(1)}, u32[]{:S(2)}, u32[]{:S(2)}) collective-permute-start(f32[2,128,16,128]{3,2,1,0:T(8,128)S(1)} %add.96), channel_id=1, source_target_pairs={{0,4},{1,5},{2,6},{3,7},{4,0},{5,1},{6,2},{7,3},{8,12},{9,13},{10,... | collective-permute-start | bytes 6291464 | tf_op jit(solution)/shard_map/ppermute | solution.py:11
  522.2 194.2 %collective-permute-start.5 = (f32[2,128,16,128]{3,2,1,0:T(8,128)S(1)}, f32[2,128,16,128]{3,2,1,0:T(8,128)}, u32[]{:S(2)}, u32[]{:S(2)}) collective-permute-start(f32[2,128,16,128]{3,2,1,0:T(8,128)S(1)} %add.97), channel_id=1, source_target_pairs={{0,8},{1,9},{2,10},{3,11},{4,12},{5,13},{6,14},{7,15},{8,0},{9,1},... | collective-permute-start | bytes 6291464 | tf_op jit(solution)/shard_map/ppermute | solution.py:11
